TPU v7x, 32 devices: a whole 2x2x4 slice. The times are simulated.
32 devices in a mesh: grp: 2 (over y), feat: 4 (over z), samp: 4 (over x, core).
Axes of the slice: x: 2, y: 2, z: 4, core: 2. Of those that a mesh axis runs over, the one named last changes fastest.
Arguments:
- embeddings: bfloat16 [8192, 1024], P(('grp', 'samp')), parts along dimension 0, may hold values from -6 to 6
- sign_bits: int32 [4096], P('feat'), may hold values 0 or 1
- perms: int32 [4, 1024], P('feat'), may hold values from 0 to 1023, each once within a row
- gauss: float32 [4096], P('feat'), may hold values from -4 to 4
- scale: float32 [4096], P('feat'), may hold values from 0.5 to 2
- phase: float32 [4096], P('feat'), may hold values from -3.140625 to 3.140625
- basis: float32 [128, 4096], P('grp', 'feat'), parts along dimension 0, may hold values from -40 to 40
Outputs:
- basis_out: float32 [128, 4096], P('grp', 'feat'), parts along dimension 0
- projections: float32 [128, 4096], P('grp', 'samp'), parts along dimension 0
There are 2 independent parts, one for each index of `grp`. A program takes and returns all parts, laid end to end along the dimension named above; an argument that names none is the same for every part. Nothing has to cross between parts.
Inputs may be any that keep to these rules, and one draw needn't show every extreme that they name: Each row of perms names every number of 0 to 1023 once.
All inputs are finite; a program needn't handle non-finite values. No bound on the sum of `sign_bits` on one device may be relied on, other than what follows from the above.
Results may differ from a plain program's by a relative error of at most 0.0057.
Values sent between devices are 32-bit elements; how exact they have to be, the bound alone decides.
A program may use at most 64 MiB of HBM per device.

v0:
```python
import math
import jax
import jax.numpy as jnp
from jax import lax
from jax.sharding import PartitionSpec as P


def sylvester(width):
    indices = lax.iota(jnp.int32, width)
    parity = jnp.zeros((width, width), jnp.int32)
    for position in range(width.bit_length() - 1):
        row_bits = jnp.right_shift(indices[:, None], position) & 1
        col_bits = jnp.right_shift(indices[None, :], position) & 1
        parity = parity + row_bits * col_bits
    return jnp.where(parity % 2 == 0, 1.0, -1.0).astype(jnp.bfloat16)


def cholesky_step(grown, total):
    local_gram = jnp.dot(grown, grown.T, precision=lax.Precision.HIGHEST)
    gram = lax.psum(local_gram, "feat")
    lower = jnp.linalg.cholesky(gram / total)
    return jax.scipy.linalg.solve_triangular(lower, grown, lower=True)


def local(embeddings, sign_bits, perms, gauss, scale, phase, basis):
    width = embeddings.shape[1]
    rows = embeddings.shape[0]
    table = sylvester(width)
    features_total = width * lax.axis_size("feat")
    span_total = rows * lax.axis_size("samp")
    signs = (2 * sign_bits - 1).astype(jnp.bfloat16)
    first = jnp.dot(embeddings * signs, table, preferred_element_type=jnp.float32).astype(
        jnp.bfloat16
    )
    reorder = (lax.iota(jnp.int32, width)[:, None] == perms[0][None, :]).astype(jnp.bfloat16)
    picked = jnp.dot(first, reorder, preferred_element_type=jnp.float32)
    mixed = (picked * gauss).astype(jnp.bfloat16)
    freq = jnp.dot(mixed, table, preferred_element_type=jnp.float32) * scale / width + phase
    features = (math.sqrt(2.0) * jnp.cos(freq)).astype(jnp.bfloat16)
    basis_low = basis.astype(jnp.bfloat16)
    partial_scores = lax.dot_general(
        basis_low, features, (((1,), (1,)), ((), ())), preferred_element_type=jnp.float32
    )
    summed = lax.psum(partial_scores, "feat")
    projections = summed / math.sqrt(features_total)
    proj_low = projections.astype(jnp.bfloat16)
    update_part = jnp.dot(proj_low, features, preferred_element_type=jnp.float32)
    update = lax.psum(update_part, "samp")
    grown = basis + update / math.sqrt(span_total)
    basis_out = cholesky_step(grown, features_total)
    return (basis_out, projections)


def solution(mesh):
    placed = (
        P(("grp", "samp"), None),
        P("feat"),
        P("feat", None),
        P("feat"),
        P("feat"),
        P("feat"),
        P("grp", "feat"),
    )
    return jax.shard_map(
        local,
        mesh=mesh,
        in_specs=placed,
        out_specs=(P("grp", "feat"), P("grp", "samp")),
        check_vma=False,
    )
```

profile of v0, /device:TPU:0, one launch (start us, length us, event | category | flops | bytes accessed | tf_op | source)
XLA Modules:
  0.0 159.9 jit_solution(12361996061334306493)
XLA Ops:
  7.2 0.0 all-reduce.3.cloned.1.call-start
  7.3 0.7 add_convert_fusion
  8.0 1.5 iota_compare_fusion.7
  9.5 0.0 copy-start.2
  9.5 0.0 copy-start.3
  9.5 0.0 copy-start.4
  9.5 12.2 %fusion.2 = f32[1024,1024]{1,0:T(8,128)} fusion(bf16[1024,1024]{1,0:T(8,128)(2,1)} %param.7, bf16[1024]{0:T(1024)(128)(2,1)S(1)} %add_convert_fusion, s32[1024]{0:T(1024)S(1)} %get-tuple-element.2, s32[1024]{0:T(1024)S(1)} %get-tuple-element.3, s32[1024]{0:T(1024)S(1)} %get-tuple-element.4, s32[1024]{0:T(1024)S(1)} %get-tuple-element.5, ...), kind=kOutput, calls=%fused_computation.9 | convolution fusion | flops 4331667456 | bytes 7383040 | tf_op jit(solution)/shard_map/dot_general | solution.py:36
  21.7 0.0 copy-done.2
  21.7 0.0 copy-done.3
  21.7 0.0 copy-done.4
  21.7 0.0 copy-start
  21.7 22.2 %multiply_convert_fusion = bf16[1024,1024]{1,0:T(8,128)(2,1)S(1)} fusion(f32[1024,1024]{1,0:T(8,128)} %fusion.2, f32[1024]{0:T(1024)S(1)} %copy-done.2, f32[1024]{0:T(1024)S(1)} %copy-done.3, f32[1024]{0:T(1024)S(1)} %copy-done.4, s32[1024]{0:T(1024)S(1)} %get-tuple-element.2, s32[1024]{0:T(1024)S(1)} %get-tuple-element.3, s32[1024]{0:T(1024)S(1)} %get-tuple-element.4, ...), kind=kOutput, calls=%fused_computation.5 | convolution fusion | flops 2189426688 | bytes 6344704 | tf_op jit(solution)/shard_map/dot_general | solution.py:38
  44.0 0.0 copy-done
  44.0 1.5 convolution_bitcast_fusion
  45.4 0.0 all-reduce.3.cloned.1.call-update
  45.5 0.0 all-reduce.5.cloned.1.call-start
  45.5 38.1 %all-reduce.3.cloned.1.call-done = f32[64,1024]{1,0:T(8,128)} async-done(((f32[64,1024]{1,0:T(8,128)}), f32[64,1024]{1,0:T(8,128)}) %all-reduce.3.cloned.1.call-update) | async-done | bytes 262160 | tf_op jit(solution)/shard_map/psum | solution.py:44
  83.6 1.0 broadcast_multiply_fusion
  84.6 0.0 copy-start.1
  84.6 1.2 fusion.14
  85.8 0.0 all-reduce.5.cloned.1.call-update
  85.8 32.5 %all-reduce.5.cloned.1.call-done = f32[64,1024]{1,0:T(8,128)} async-done(((f32[64,1024]{1,0:T(8,128)}), f32[64,1024]{1,0:T(8,128)}) %all-reduce.5.cloned.1.call-update) | async-done | bytes 262160 | tf_op jit(solution)/shard_map/psum | solution.py:48
  118.4 1.4 fusion.18
  119.8 19.0 %psum.23 = f32[64,64]{0,1:T(8,128)S(1)} all-reduce(f32[64,64]{0,1:T(8,128)S(1)} %fusion.18), channel_id=1, replica_groups=mesh['grp'=2,'feat'=4,'samp'=4] {'feat'}, use_global_device_ids=true, to_apply=%region_2.3 | all-reduce | flops 4096 | bytes 32768 | tf_op jit(solution)/shard_map/psum | solution.py:20
  138.8 0.1 copy.10
  138.9 5.8 %cholesky.16 = f32[64,64]{1,0:T(8,128)S(1)} custom-call(f32[64,64]{1,0:T(8,128)S(1)} %fusion.21), custom_call_target="Cholesky" | custom-call | tf_op jit(solution)/shard_map/jit(cholesky)/cholesky | solution.py:21
  144.7 0.6 compare_reduce_fusion
  145.4 0.7 fusion.19
  146.1 4.9 %custom-call.7 = f32[1,64,64]{1,2,0:T(8,128)S(1)} custom-call(f32[1,64,64]{2,1,0:T(8,128)S(1)} %fusion.19), custom_call_target="InvertDiagBlocksLowerTriangular" | custom-call | tf_op jit(solution)/shard_map/jit(_solve_triangular)/triangular_solve | solution.py:22
  150.9 2.1 %fusion.17 = f32[64,1024]{1,0:T(8,128)} fusion(f32[64,1024]{1,0:T(8,128)S(1)} %copy-done, f32[64,1024]{1,0:T(8,128)} %all-reduce.5.cloned.1.call-done, f32[1,64,64]{1,2,0:T(8,128)S(1)} %custom-call.7), kind=kOutput, calls=%fused_computation.22 | convolution fusion | flops 50462720 | bytes 802816 | tf_op jit(solution)/shard_map/jit(_solve_triangular)/triangular_solve | solution.py:22
  153.0 0.0 copy-done.1
  (8 shorter events, 0.1 us)
Async XLA Ops:
  7.2 76.5 %all-reduce.3.cloned.1.call-start = ((), (), s32[]{:S(2)}) async-start(), calls=%async_computation | async-start | bytes 524288 | tf_op jit(solution)/shard_map/psum | solution.py:44
  9.5 12.3 %copy-start.2 = (f32[1024]{0:T(1024)S(1)}, f32[1024]{0:T(1024)}, u32[]{:S(2)}) copy-start(f32[1024]{0:T(1024)} %param.12) | copy-start | bytes 12292
  9.5 12.3 %copy-start.3 = (f32[1024]{0:T(1024)S(1)}, f32[1024]{0:T(1024)}, u32[]{:S(2)}) copy-start(f32[1024]{0:T(1024)} %param.11) | copy-start | bytes 12292
  9.5 12.3 %copy-start.4 = (f32[1024]{0:T(1024)S(1)}, f32[1024]{0:T(1024)}, u32[]{:S(2)}) copy-start(f32[1024]{0:T(1024)} %param.10) | copy-start | bytes 12292
  21.7 22.2 %copy-start = (f32[64,1024]{1,0:T(8,128)S(1)}, f32[64,1024]{1,0:T(8,128)}, u32[]{:S(2)}) copy-start(f32[64,1024]{1,0:T(8,128)} %param.13) | copy-start | bytes 786436
  45.5 72.9 %all-reduce.5.cloned.1.call-start = ((), (), s32[]{:S(2)}) async-start(), calls=%async_computation.1 | async-start | bytes 524288 | tf_op jit(solution)/shard_map/psum | solution.py:48
  84.6 68.4 %copy-start.1 = (f32[64,1024]{1,0:T(8,128)}, f32[64,1024]{1,0:T(8,128)S(1)}, u32[]{:S(2)}) copy-start(f32[64,1024]{1,0:T(8,128)S(1)} %broadcast_multiply_fusion) | copy-start | bytes 786436
Sparse Core Ops, SparseCore 0:
  45.6 37.9 all-reduce.2
  86.6 31.6 all-reduce.4
where the time goes:
time: 160 us
  waiting for transfers between devices  70.7 us (44%)
  matrix products  40.6 us (25%)
  blocking collectives  19 us (12%)
  other arithmetic  15.3 us (10%)
  between operations  14.2 us (9%)
    psum x1, waiting for transfers between devices, local(): summed = lax.psum(partial_scores, 'feat')  38.1 us
    psum x1, waiting for transfers between devices, local(): update = lax.psum(update_part, 'samp')  32.5 us
    dot_general x1, matrix products, local(): jnp.dot(mixed, table, preferred_element_type=jnp.float32) * scale / width  22.2 us
    psum x1, blocking collectives, cholesky_step(): gram = lax.psum(local_gram, 'feat')  19 us
    dot_general x1, matrix products, local(): picked = jnp.dot(first, reorder, preferred_element_type=jnp.float32)  12.2 us
    another operation x3, other arithmetic, cholesky_step(): lower = jnp.linalg.cholesky(gram / total)  6.52 us
    another operation x2, other arithmetic, cholesky_step(): return jax.scipy.linalg.solve_triangular(lower, grown, lower=True)  5.55 us
  transfers between devices with their start and end apart: 2, of which 2 were waited for; matrix products, arithmetic and copies ran while one was open for 0% of the time, Pallas kernels for 0%

commit v1 on v0

--- a/solution.py
+++ b/solution.py
@@ -41,7 +41,11 @@
     partial_scores = lax.dot_general(
         basis_low, features, (((1,), (1,)), ((), ())), preferred_element_type=jnp.float32
     )
-    summed = lax.psum(partial_scores, "feat")
+    n_dev = lax.axis_size("feat")
+    summed, far = (partial_scores, 1)
+    while far < n_dev:
+        summed = summed + lax.ppermute(summed, "feat", [(i, i ^ far) for i in range(n_dev)])
+        far = 2 * far
     projections = summed / math.sqrt(features_total)
     proj_low = projections.astype(jnp.bfloat16)
     update_part = jnp.dot(proj_low, features, preferred_element_type=jnp.float32)

time: 160 us -> 144 us (0.900)
  waiting for transfers between devices: 70.7 us -> 50.7 us
  starting transfers between devices: 0.08 us -> 5.94 us
    psum x1 -> x0, waiting for transfers between devices: 38.1 us -> none  [local(): summed = lax.psum(partial_scores, 'feat')]
    ppermute x0 -> x2, waiting for transfers between devices: none -> 17.6 us  [local(): lax.ppermute(summed, 'feat', [(i, i ^ far) for i in range(n_dev)])]
    ppermute x0 -> x2, starting transfers between devices: none -> 5.9 us  [local(): lax.ppermute(summed, 'feat', [(i, i ^ far) for i in range(n_dev)])]
  transfers between devices with their start and end apart: 2 -> 3, of which waited for: 2 -> 3; matrix products, arithmetic and copies ran while one was open for 0% -> 0% of each run, Pallas kernels for 0% -> 0%
where the time goes in v1:
time: 144 us
  waiting for transfers between devices  50.7 us (35%)
  matrix products  39.9 us (28%)
  blocking collectives  19 us (13%)
  other arithmetic  14.4 us (10%)
  between operations  14.2 us (10%)
  starting transfers between devices  5.94 us (4%)
    psum x1, waiting for transfers between devices, local(): update = lax.psum(update_part, 'samp')  33.1 us
    dot_general x1, matrix products, local(): jnp.dot(mixed, table, preferred_element_type=jnp.float32) * scale / width  22.2 us
    psum x1, blocking collectives, cholesky_step(): gram = lax.psum(local_gram, 'feat')  19 us
    ppermute x2, waiting for transfers between devices, local(): lax.ppermute(summed, 'feat', [(i, i ^ far) for i in range(n_dev)])  17.6 us
    dot_general x1, matrix products, local(): picked = jnp.dot(first, reorder, preferred_element_type=jnp.float32)  12.2 us
    another operation x3, other arithmetic, cholesky_step(): lower = jnp.linalg.cholesky(gram / total)  6.52 us
    ppermute x2, starting transfers between devices, local(): lax.ppermute(summed, 'feat', [(i, i ^ far) for i in range(n_dev)])  5.9 us
    another operation x2, other arithmetic, cholesky_step(): return jax.scipy.linalg.solve_triangular(lower, grown, lower=True)  5.55 us
  transfers between devices with their start and end apart: 3, of which 3 were waited for; matrix products, arithmetic and copies ran while one was open for 0% of the time, Pallas kernels for 0%

profile of v1, /device:TPU:0, one launch (start us, length us, event | category | flops | bytes accessed | tf_op | source)
XLA Modules:
  0.0 144.1 jit_solution(5246537832076050729)
XLA Ops:
  7.2 0.0 all-reduce.2.cloned.1.call-start
  7.3 0.7 add_convert_fusion
  8.0 1.5 %iota_compare_fusion.7 = pred[1024,1024]{1,0:T(32,128)(4,1)S(1)} fusion(s32[1024]{0:T(1024)} %bitcast.15), kind=kLoop, calls=%fused_computation.7.clone.clone.2 | loop fusion | flops 1048576 | bytes 1052672 | tf_op jit(solution)/shard_map/dot_general | solution.py:36
  9.5 0.0 copy-start.2
  9.5 0.0 copy-start.3
  9.5 0.0 copy-start.4
  9.5 12.2 %fusion.2 = f32[1024,1024]{1,0:T(8,128)} fusion(bf16[1024,1024]{1,0:T(8,128)(2,1)} %param.7, bf16[1024]{0:T(1024)(128)(2,1)S(1)} %add_convert_fusion, s32[1024]{0:T(1024)S(1)} %get-tuple-element.2, s32[1024]{0:T(1024)S(1)} %get-tuple-element.3, s32[1024]{0:T(1024)S(1)} %get-tuple-element.4, s32[1024]{0:T(1024)S(1)} %get-tuple-element.5, ...), kind=kOutput, calls=%fused_computation.9 | convolution fusion | flops 4331667456 | bytes 7383040 | tf_op jit(solution)/shard_map/dot_general | solution.py:36
  21.7 0.0 copy-done.2
  21.7 0.0 copy-done.3
  21.7 0.0 copy-done.4
  21.7 0.0 copy-start
  21.8 22.2 %multiply_convert_fusion = bf16[1024,1024]{1,0:T(8,128)(2,1)S(1)} fusion(f32[1024,1024]{1,0:T(8,128)} %fusion.2, f32[1024]{0:T(1024)S(1)} %copy-done.2, f32[1024]{0:T(1024)S(1)} %copy-done.3, f32[1024]{0:T(1024)S(1)} %copy-done.4, s32[1024]{0:T(1024)S(1)} %get-tuple-element.2, s32[1024]{0:T(1024)S(1)} %get-tuple-element.3, s32[1024]{0:T(1024)S(1)} %get-tuple-element.4, ...), kind=kOutput, calls=%fused_computation.5 | convolution fusion | flops 2189426688 | bytes 6344704 | tf_op jit(solution)/shard_map/dot_general | solution.py:38
  44.0 0.0 copy-done
  44.0 0.8 convolution_bitcast_fusion
  44.7 3.1 %collective-permute-start = (f32[64,1024]{1,0:T(8,128)S(1)}, f32[64,1024]{1,0:T(8,128)S(1)}, u32[]{:S(2)}, u32[]{:S(2)}) collective-permute-start(f32[64,1024]{1,0:T(8,128)S(1)} %convolution_bitcast_fusion), channel_id=1, source_target_pairs={{0,4},{4,0},{8,12},{12,8},{1,5},{5,1},{9,13},{13,9},{2,6},{6,2},{1... | collective-permute-start | bytes 786440 | tf_op jit(solution)/shard_map/ppermute | solution.py:47
  47.8 6.3 %collective-permute-done = f32[64,1024]{1,0:T(8,128)S(1)} collective-permute-done((f32[64,1024]{1,0:T(8,128)S(1)}, f32[64,1024]{1,0:T(8,128)S(1)}, u32[]{:S(2)}, u32[]{:S(2)}) %collective-permute-start) | collective-permute-done | bytes 262176 | tf_op jit(solution)/shard_map/ppermute | solution.py:47
  54.2 2.8 %collective-permute-start.1 = (f32[64,1024]{1,0:T(8,128)S(1)}, f32[64,1024]{1,0:T(8,128)S(1)}, u32[]{:S(2)}, u32[]{:S(2)}) collective-permute-start(f32[64,1024]{1,0:T(8,128)S(1)} %add.99), channel_id=1, source_target_pairs={{0,8},{4,12},{8,0},{12,4},{1,9},{5,13},{9,1},{13,5},{2,10},{6,14},... | collective-permute-start | bytes 786440 | tf_op jit(solution)/shard_map/ppermute | solution.py:47
  57.0 11.3 %collective-permute-done.1 = f32[64,1024]{1,0:T(8,128)S(1)} collective-permute-done((f32[64,1024]{1,0:T(8,128)S(1)}, f32[64,1024]{1,0:T(8,128)S(1)}, u32[]{:S(2)}, u32[]{:S(2)}) %collective-permute-start.1) | collective-permute-done | bytes 262176 | tf_op jit(solution)/shard_map/ppermute | solution.py:47
  68.3 0.0 copy-start.1
  68.3 1.2 fusion.14
  69.5 0.0 all-reduce.2.cloned.1.call-update
  69.5 33.1 %all-reduce.2.cloned.1.call-done = f32[64,1024]{1,0:T(8,128)} async-done(((f32[64,1024]{1,0:T(8,128)}), f32[64,1024]{1,0:T(8,128)}) %all-reduce.2.cloned.1.call-update) | async-done | bytes 262160 | tf_op jit(solution)/shard_map/psum | solution.py:52
  102.6 1.4 fusion.18
  104.0 19.0 %psum.15 = f32[64,64]{0,1:T(8,128)S(1)} all-reduce(f32[64,64]{0,1:T(8,128)S(1)} %fusion.18), channel_id=1, replica_groups=mesh['grp'=2,'feat'=4,'samp'=4] {'feat'}, use_global_device_ids=true, to_apply=%region_1.2 | all-reduce | flops 4096 | bytes 32768 | tf_op jit(solution)/shard_map/psum | solution.py:20
  123.0 0.1 copy.10
  123.1 5.8 %cholesky.16 = f32[64,64]{1,0:T(8,128)S(1)} custom-call(f32[64,64]{1,0:T(8,128)S(1)} %fusion.21), custom_call_target="Cholesky" | custom-call | tf_op jit(solution)/shard_map/jit(cholesky)/cholesky | solution.py:21
  129.0 0.6 compare_reduce_fusion
  129.6 0.7 fusion.19
  130.3 4.9 %custom-call.7 = f32[1,64,64]{1,2,0:T(8,128)S(1)} custom-call(f32[1,64,64]{2,1,0:T(8,128)S(1)} %fusion.19), custom_call_target="InvertDiagBlocksLowerTriangular" | custom-call | tf_op jit(solution)/shard_map/jit(_solve_triangular)/triangular_solve | solution.py:22
  135.2 2.1 %fusion.17 = f32[64,1024]{1,0:T(8,128)} fusion(f32[64,1024]{1,0:T(8,128)S(1)} %copy-done, f32[64,1024]{1,0:T(8,128)} %all-reduce.2.cloned.1.call-done, f32[1,64,64]{1,2,0:T(8,128)S(1)} %custom-call.7), kind=kOutput, calls=%fused_computation.22 | convolution fusion | flops 50462720 | bytes 802816 | tf_op jit(solution)/shard_map/jit(_solve_triangular)/triangular_solve | solution.py:22
  137.3 0.0 copy-done.1
  (10 shorter events, 0.1 us)
Async XLA Ops:
  7.2 95.4 %all-reduce.2.cloned.1.call-start = ((), (), s32[]{:S(2)}) async-start(), calls=%async_computation | async-start | bytes 524288 | tf_op jit(solution)/shard_map/psum | solution.py:52
  9.5 12.3 %copy-start.2 = (f32[1024]{0:T(1024)S(1)}, f32[1024]{0:T(1024)}, u32[]{:S(2)}) copy-start(f32[1024]{0:T(1024)} %param.12) | copy-start | bytes 12292
  9.5 12.3 %copy-start.3 = (f32[1024]{0:T(1024)S(1)}, f32[1024]{0:T(1024)}, u32[]{:S(2)}) copy-start(f32[1024]{0:T(1024)} %param.11) | copy-start | bytes 12292
  9.5 12.3 %copy-start.4 = (f32[1024]{0:T(1024)S(1)}, f32[1024]{0:T(1024)}, u32[]{:S(2)}) copy-start(f32[1024]{0:T(1024)} %param.10) | copy-start | bytes 12292
  21.7 22.2 %copy-start = (f32[64,1024]{1,0:T(8,128)S(1)}, f32[64,1024]{1,0:T(8,128)}, u32[]{:S(2)}) copy-start(f32[64,1024]{1,0:T(8,128)} %param.13) | copy-start | bytes 786436
  44.7 9.4 %collective-permute-start = (f32[64,1024]{1,0:T(8,128)S(1)}, f32[64,1024]{1,0:T(8,128)S(1)}, u32[]{:S(2)}, u32[]{:S(2)}) collective-permute-start(f32[64,1024]{1,0:T(8,128)S(1)} %convolution_bitcast_fusion), channel_id=1, source_target_pairs={{0,4},{4,0},{8,12},{12,8},{1,5},{5,1},{9,13},{13,9},{2,6},{6,2},{1... | collective-permute-start | bytes 786440 | tf_op jit(solution)/shard_map/ppermute | solution.py:47
  54.2 14.1 %collective-permute-start.1 = (f32[64,1024]{1,0:T(8,128)S(1)}, f32[64,1024]{1,0:T(8,128)S(1)}, u32[]{:S(2)}, u32[]{:S(2)}) collective-permute-start(f32[64,1024]{1,0:T(8,128)S(1)} %add.99), channel_id=1, source_target_pairs={{0,8},{4,12},{8,0},{12,4},{1,9},{5,13},{9,1},{13,5},{2,10},{6,14},... | collective-permute-start | bytes 786440 | tf_op jit(solution)/shard_map/ppermute | solution.py:47
  68.3 69.0 %copy-start.1 = (f32[64,1024]{1,0:T(8,128)}, f32[64,1024]{1,0:T(8,128)S(1)}, u32[]{:S(2)}) copy-start(f32[64,1024]{1,0:T(8,128)S(1)} %add_multiply_fusion) | copy-start | bytes 786436
Sparse Core Ops, SparseCore 0:
  69.6 32.9 all-reduce.1
